TPU v7x, 32 devices: a whole 2x2x4 slice. The times are simulated.
32 devices in a mesh: light: 4 (over z), view: 8 (over y, x, core).
Axes of the slice: x: 2, y: 2, z: 4, core: 2. Of those that a mesh axis runs over, the one named last changes fastest.
Arguments:
- density: float32 [8, 128, 1024], P('light', 'view'), may hold values from 0 to 1
- colour: bfloat16 [3, 8, 128, 1024], P(None, 'light', 'view'), may hold values from 0 to 1
- absorb: float32 [3], replicated, may hold values from 0.3 to 3
- light_in: float32 [3, 128, 1024], P(None, 'view'), may hold values from 0.5 to 1.5
Outputs:
- image: float32 [4, 8, 1024], P(None, 'light', 'view')
All inputs are finite; a program needn't handle non-finite values.
Results may differ from a plain program's by a relative error of at most 0.0003.
Values sent between devices are 32-bit elements; how exact they have to be, the bound alone decides.
A program may use at most 64 MiB of HBM per device.

v0:
```python
import functools

import jax
import jax.numpy as jnp
from jax import lax
from jax.experimental import pallas as pl
from jax.experimental.pallas import tpu as pltpu
from jax.sharding import PartitionSpec as P

view_scale = 0.25
blur_center = 0.5
blur_edge = 0.1
blur_corner = 0.025

MESH = pl.DeviceIdType.MESH


def opacity_of(values):
    return 0.01 * values + 0.03 * values * values * values


def kernel(
    lights,
    views,
    density_hbm,
    colour_hbm,
    absorb_ref,
    light_hbm,
    out_ref,
    density_ref,
    colour_ref,
    light_ref,
    load_sem,
    first,
    first_top,
    first_bottom,
    first_above,
    first_below,
    first_opacity,
    first_send,
    first_recv,
    seed_above,
    seed_below,
    seed_recv,
    plane_ref,
    wide_top,
    wide_bottom,
    wide_send,
    wide_recv,
    own,
    above,
    below,
    passed,
    edge_top,
    edge_bottom,
    seed_top,
    seed_bottom,
    dens_top,
    dens_bottom,
    dens_above,
    dens_below,
    ring_opacity,
    weight,
    rows_a,
    rows_b,
    send_a,
    send_b,
    got_a,
    got_b,
    own_send,
    own_recv,
    edge_send,
    edge_recv,
    seed_send,
    dens_send,
    dens_recv,
    a_send,
    a_recv,
    b_send,
    b_recv,
):
    l = lax.axis_index("light")
    v = lax.axis_index("view")
    slices, height, width = density_ref.shape
    channels = light_ref.shape[0]
    spare = plane_ref.shape[0] - height
    reach2 = seed_above.shape[1]
    cols = out_ref.shape[1]
    has_above = v > 0
    has_below = v < views - 1
    has_next = l < lights - 1
    is_first = l == 0
    even = lax.rem(l, 2) == 0
    odd = lax.rem(l, 2) == 1
    gives = (is_first | odd) & has_next
    takes = (l == 1) | (even & (l > 1))
    jumps = even & (l < lights - 2)
    steps = even & (l > 1) & has_next

    barrier = pltpu.get_barrier_semaphore()

    def greet(dl, dv):
        pl.semaphore_signal(
            barrier, inc=1, device_id={"light": l + dl, "view": v + dv}, device_id_type=MESH
        )

    for step in range(1, views):
        pl.semaphore_signal(
            barrier,
            inc=1,
            device_id={"light": l, "view": lax.rem(v + step, views)},
            device_id_type=MESH,
        )
    for dl in (-2, -1, 1, 2):
        l_ok = l >= -dl if dl < 0 else l < lights - dl
        if abs(dl) == 2:
            l_ok = l_ok & even

        @pl.when(l_ok)
        def _():
            greet(dl, 0)

        for dv in (-1, 1):

            @pl.when(l_ok & (has_above if dv < 0 else has_below))
            def _():
                greet(dl, dv)

    one = jnp.int32(1)
    zero = jnp.int32(0)
    lines = jnp.where(l > 0, one, zero) + jnp.where(has_next, one, zero)
    lines = lines + jnp.where(even & (l > 1), one, zero) + jnp.where(jumps, one, zero)
    sides = one + jnp.where(has_above, one, zero) + jnp.where(has_below, one, zero)

    loads = [
        pltpu.make_async_copy(src, dst, load_sem.at[i])
        for i, (src, dst) in enumerate(
            ((density_hbm, density_ref), (light_hbm, light_ref), (colour_hbm, colour_ref))
        )
    ]
    for load in loads:
        load.start()

    @pl.when(jnp.logical_not(has_above))
    def _():
        above[...] = jnp.zeros_like(above)
        dens_above[...] = jnp.zeros_like(dens_above)
        first_above[...] = jnp.zeros_like(first_above)
        seed_above[...] = jnp.zeros_like(seed_above)

    @pl.when(jnp.logical_not(has_below))
    def _():
        below[...] = jnp.zeros_like(below)
        dens_below[...] = jnp.zeros_like(dens_below)
        first_below[...] = jnp.zeros_like(first_below)
        seed_below[...] = jnp.zeros_like(seed_below)

    loads[0].wait()
    dens_top[...] = density_ref[:, :slices, :]
    dens_bottom[...] = density_ref[:, height - slices :, :]

    @pl.when(gives)
    def _():
        first_top[...] = density_ref[:, :reach2, :]
        first_bottom[...] = density_ref[:, height - reach2 :, :]

    loads[1].wait()

    @pl.when(l <= 1)
    def _():
        seed_top[...] = light_ref[:, :reach2, :]
        seed_bottom[...] = light_ref[:, height - reach2 :, :]

    pl.semaphore_wait(barrier, views - 1 + lines * sides)

    def copy(src, dst, send, recv, to_l, to_v):
        return pltpu.make_async_remote_copy(
            src_ref=src,
            dst_ref=dst,
            send_sem=send,
            recv_sem=recv,
            device_id={"light": to_l, "view": to_v},
            device_id_type=MESH,
        )

    def dens_up():
        return copy(dens_top, dens_below, dens_send.at[0], dens_recv.at[0], l, v - 1)

    def dens_down():
        return copy(dens_bottom, dens_above, dens_send.at[1], dens_recv.at[1], l, v + 1)

    def edge_up(c):
        return copy(
            edge_top.at[c], below.at[c], edge_send.at[0, c], edge_recv.at[0, c], l + 1, v - 1
        )

    def edge_down(c):
        return copy(
            edge_bottom.at[c], above.at[c], edge_send.at[1, c], edge_recv.at[1, c], l + 1, v + 1
        )

    def wide_up(c):
        return copy(
            wide_top.at[c], seed_below.at[c], wide_send.at[0, c], wide_recv.at[0, c], l + 2, v - 1
        )

    def wide_down(c):
        return copy(
            wide_bottom.at[c], seed_above.at[c], wide_send.at[1, c], wide_recv.at[1, c], l + 2, v + 1
        )

    def own_on(c, dl):
        return copy(passed.at[c], own.at[c], own_send.at[dl - 1, c], own_recv.at[c], l + dl, v)

    def swap(send, got, sems, recvs, step):
        target = lax.rem(v + step, views)
        return copy(send.at[target], got.at[v], sems.at[step], recvs.at[step], l, target)

    def seed_up(c):
        return copy(
            seed_top.at[c], seed_below.at[c], seed_send.at[0, c], seed_recv.at[0, c], l, v - 1
        )

    def seed_down(c):
        return copy(
            seed_bottom.at[c], seed_above.at[c], seed_send.at[1, c], seed_recv.at[1, c], l, v + 1
        )

    def first_up(s):
        return copy(
            first_top.at[s], first_below.at[s], first_send.at[0, s], first_recv.at[0, s], l + 1, v - 1
        )

    def first_down(s):
        return copy(
            first_bottom.at[s], first_above.at[s], first_send.at[1, s], first_recv.at[1, s], l + 1, v + 1
        )

    def first_on(s):
        return copy(
            density_hbm.at[s], first.at[s], first_send.at[2, s], first_recv.at[2, s], l + 1, v
        )

    @pl.when(has_above)
    def _():
        dens_up().start()

    @pl.when(has_below)
    def _():
        dens_down().start()

    for c in range(channels):

        @pl.when((l <= 1) & has_above)
        def _():
            seed_up(c).start()

        @pl.when((l <= 1) & has_below)
        def _():
            seed_down(c).start()

    for s in range(slices):

        @pl.when(gives & has_above)
        def _():
            first_up(s).start()

        @pl.when(gives & has_below)
        def _():
            first_down(s).start()

        @pl.when(gives)
        def _():
            first_on(s).start()

    row = lax.broadcasted_iota(jnp.int32, (height, width), 0)
    for s in range(slices):
        opacity = opacity_of(density_ref[s])
        ring_opacity[s, :height, :] = opacity
        alpha = view_scale * opacity
        run = 1.0 - alpha
        reach = 1
        while reach < height:
            run = run * jnp.where(row >= reach, pltpu.roll(run, reach, 0), 1.0)
            reach *= 2
        before = jnp.where(row >= 1, pltpu.roll(run, 1, 0), 1.0)
        weight[0, s] = before * alpha
        last = run[height - 1 :, :]
        for c in range(channels + 1):
            place = c * slices + s
            rows_b[place : place + 1, :] = last
        place = channels * slices + s
        rows_a[place : place + 1, :] = 1.0 - last
    for block in range(views):
        send_b[block] = rows_b[:, block * cols : (block + 1) * cols]

    for step in range(1, views):
        swap(send_b, got_b, b_send, b_recv, step).start()
    loads[2].wait()

    for s in range(slices):
        base = weight[0, s]
        for c in reversed(range(channels)):
            weight[c, s] = base * colour_ref[c, s].astype(jnp.float32)

    @pl.when(has_above)
    def _():
        dens_down().wait_recv()

    @pl.when(has_below)
    def _():
        dens_up().wait_recv()

    for s in range(slices):
        ring_opacity[s, height:, :] = jnp.zeros((spare, width), jnp.float32)
        ring_opacity[s, height : height + slices, :] = opacity_of(dens_below[s])
        ring_opacity[s, height + spare - slices :, :] = opacity_of(dens_above[s])
    plane_ref[height:, :] = jnp.zeros((spare, width), jnp.float32)

    ring_row = lax.broadcasted_iota(jnp.int32, (height + spare, width), 0)
    column = lax.broadcasted_iota(jnp.int32, (height + spare, width), 1)
    not_left = column > 0
    not_right = column < width - 1
    low = jnp.where(has_below, height + spare // 2, height)
    high = jnp.where(has_above, height + spare // 2, height + spare)
    inside = (ring_row < low) | (ring_row >= high)

    def blur(p):
        across = jnp.where(not_left, pltpu.roll(p, 1, 1), 0.0) + jnp.where(
            not_right, pltpu.roll(p, width - 1, 1), 0.0
        )
        middle = blur_center * p + blur_edge * across
        side = blur_edge * p + blur_corner * across
        total = height + spare
        return middle + (pltpu.roll(side, 1, 0) + pltpu.roll(side, total - 1, 0))

    for s in range(slices):

        @pl.when(takes & has_above)
        def _():
            first_down(s).wait_recv()

        @pl.when(takes & has_below)
        def _():
            first_up(s).wait_recv()

        @pl.when(takes)
        def _():
            first_on(s).wait_recv()
            first_opacity[s, :height, :] = opacity_of(first[s])
            first_opacity[s, height:, :] = jnp.zeros((spare, width), jnp.float32)
            first_opacity[s, height : height + reach2, :] = opacity_of(first_below[s])
            first_opacity[s, height + spare - reach2 :, :] = opacity_of(first_above[s])

    for c in range(channels):
        decay = absorb_ref[c]

        @pl.when((l <= 1) & has_above)
        def _():
            seed_down(c).wait_recv()

        @pl.when((l <= 1) & has_below)
        def _():
            seed_up(c).wait_recv()

        @pl.when(l > 1)
        def _():
            own_on(c, 1).wait_recv()

        @pl.when(even & (l > 1) & has_above)
        def _():
            wide_down(c).wait_recv()

        @pl.when(even & (l > 1) & has_below)
        def _():
            wide_up(c).wait_recv()

        @pl.when(odd & (l > 1) & has_above)
        def _():
            edge_down(c).wait_recv()

        @pl.when(odd & (l > 1) & has_below)
        def _():
            edge_up(c).wait_recv()

        @pl.when(l <= 1)
        def _():
            plane_ref[:height, :] = light_ref[c]

        @pl.when(l > 1)
        def _():
            plane_ref[:height, :] = own[c]

        @pl.when(even | (l == 1))
        def _():
            plane_ref[height : height + reach2, :] = seed_below[c]
            plane_ref[height + spare - reach2 :, :] = seed_above[c]

        @pl.when(odd & (l > 1))
        def _():
            plane_ref[height : height + slices, :] = below[c]
            plane_ref[height + spare - slices :, :] = above[c]

        @pl.when(takes)
        def _():
            swept = plane_ref[...]
            for s in range(slices):
                swept = blur(swept * (1.0 - decay * first_opacity[s]))
                swept = jnp.where(inside, swept, 0.0)
            plane_ref[...] = swept

        plane = plane_ref[...]
        for s in range(slices):
            lit = jnp.sum(weight[c, s] * plane[:height], axis=0, keepdims=True)
            place = c * slices + s
            rows_a[place : place + 1, :] = lit
            dimmed = plane * (1.0 - decay * ring_opacity[s])
            if s < slices - 1:
                plane = jnp.where(inside, blur(dimmed), 0.0)

        @pl.when(jumps | steps)
        def _():
            after = blur(dimmed)
            passed[c] = after[:height]
            edge_top[c] = after[:slices]
            edge_bottom[c] = after[height - slices : height]
            wide_top[c] = after[:reach2]
            wide_bottom[c] = after[height - reach2 : height]

        @pl.when(jumps & has_above)
        def _():
            wide_up(c).start()

        @pl.when(jumps & has_below)
        def _():
            wide_down(c).start()

        @pl.when(jumps)
        def _():
            own_on(c, 2).start()

        @pl.when(steps & has_above)
        def _():
            edge_up(c).start()

        @pl.when(steps & has_below)
        def _():
            edge_down(c).start()

        @pl.when(steps)
        def _():
            own_on(c, 1).start()

    for block in range(views):
        send_a[block] = rows_a[:, block * cols : (block + 1) * cols]
    for step in range(1, views):
        swap(send_a, got_a, a_send, a_recv, step).start()
    got_a[v] = send_a[v]
    got_b[v] = send_b[v]
    for step in range(1, views):
        swap(send_b, got_b, b_send, b_recv, step).wait_recv()
    for step in range(1, views):
        swap(send_a, got_a, a_send, a_recv, step).wait_recv()
    image = got_a[0]
    shade = got_b[0]
    for front in range(1, views):
        image = image + shade * got_a[front]
        if front < views - 1:
            shade = shade * got_b[front]
    out_ref[...] = image

    for step in range(1, views):
        swap(send_b, got_b, b_send, b_recv, step).wait_send()
        swap(send_a, got_a, a_send, a_recv, step).wait_send()

    @pl.when(has_above)
    def _():
        dens_up().wait_send()

    @pl.when(has_below)
    def _():
        dens_down().wait_send()

    for c in range(channels):

        @pl.when(jumps & has_above)
        def _():
            wide_up(c).wait_send()

        @pl.when(jumps & has_below)
        def _():
            wide_down(c).wait_send()

        @pl.when(jumps)
        def _():
            own_on(c, 2).wait_send()

        @pl.when(steps & has_above)
        def _():
            edge_up(c).wait_send()

        @pl.when(steps & has_below)
        def _():
            edge_down(c).wait_send()

        @pl.when(steps)
        def _():
            own_on(c, 1).wait_send()

    for c in range(channels):

        @pl.when((l <= 1) & has_above)
        def _():
            seed_up(c).wait_send()

        @pl.when((l <= 1) & has_below)
        def _():
            seed_down(c).wait_send()

    for s in range(slices):

        @pl.when(gives & has_above)
        def _():
            first_up(s).wait_send()

        @pl.when(gives & has_below)
        def _():
            first_down(s).wait_send()

        @pl.when(gives)
        def _():
            first_on(s).wait_send()


def on_device(lights, views, density, colour, absorb, light_in):
    slices, height, width = density.shape
    channels = light_in.shape[0]
    cols = width // views
    rows = (channels + 1) * slices
    spare = -(-4 * slices // 8) * 8
    reach2 = 2 * slices
    f32 = jnp.float32
    edges = pltpu.VMEM((channels, slices, width), f32)
    dens_edges = pltpu.VMEM((slices, slices, width), f32)
    plane = pltpu.VMEM((channels, height, width), f32)
    blocks = pltpu.VMEM((views, rows, cols), f32)
    dma = pltpu.SemaphoreType.DMA
    vmem = pl.BlockSpec(memory_space=pltpu.VMEM)
    hbm = pl.BlockSpec(memory_space=pl.ANY)
    first_edges = pltpu.VMEM((slices, reach2, width), f32)
    seeds = pltpu.VMEM((channels, reach2, width), f32)
    ring_slices = pltpu.VMEM((slices, height + spare, width), f32)
    image = pl.pallas_call(
        functools.partial(kernel, lights, views),
        out_shape=pltpu.VMEM((rows, cols), f32),
        in_specs=[hbm, hbm, pl.BlockSpec(memory_space=pltpu.SMEM), hbm],
        out_specs=vmem,
        scratch_shapes=[
            pltpu.VMEM(density.shape, density.dtype),
            pltpu.VMEM(colour.shape, colour.dtype),
            plane,
            dma((3,)),
            pltpu.VMEM(density.shape, density.dtype),
            first_edges,
            first_edges,
            first_edges,
            first_edges,
            ring_slices,
            dma((3, slices)),
            dma((3, slices)),
            seeds,
            seeds,
            dma((2, channels)),
            pltpu.VMEM((height + spare, width), f32),
            seeds,
            seeds,
            dma((2, channels)),
            dma((2, channels)),
            plane,
            edges,
            edges,
            plane,
            edges,
            edges,
            seeds,
            seeds,
            dens_edges,
            dens_edges,
            dens_edges,
            dens_edges,
            ring_slices,
            pltpu.VMEM((channels, slices, height, width), f32),
            pltpu.VMEM((rows, width), f32),
            pltpu.VMEM((rows, width), f32),
            blocks,
            blocks,
            blocks,
            blocks,
            dma((2, channels)),
            dma((channels,)),
            dma((2, channels)),
            dma((2, channels)),
            dma((2, channels)),
            dma((2,)),
            dma((2,)),
            dma((views,)),
            dma((views,)),
            dma((views,)),
            dma((views,)),
        ],
        compiler_params=pltpu.CompilerParams(collective_id=0, has_side_effects=True),
    )(density, colour, absorb, light_in)
    return image.reshape(channels + 1, slices, cols)


def solution(mesh):
    return jax.shard_map(
        functools.partial(on_device, mesh.shape["light"], mesh.shape["view"]),
        mesh=mesh,
        in_specs=(
            P("light", "view", None),
            P(None, "light", "view", None),
            P(),
            P(None, "view", None),
        ),
        out_specs=P(None, "light", "view"),
        check_vma=False,
    )
```

profile of v0, /device:TPU:25, one launch (start us, length us, event | category | flops | bytes accessed | tf_op | source)
XLA Modules:
  0.0 25.0 jit_solution(5305023942057058382)
XLA Ops:
  0.0 24.4 %shard_map.46 = f32[8,128]{1,0:T(8,128)S(1)} custom-call(f32[2,16,1024]{2,1,0:T(8,128)} %density_hbm.1, bf16[3,2,16,1024]{3,2,1,0:T(8,128)(2,1)} %colour_hbm.1, f32[3]{0:T(128)} %absorb_ref.1, f32[3,16,1024]{2,1,0:T(8,128)} %light_hbm.1), custom_call_target="tpu_custom_call" | custom-call | tf_op jit(solution)/shard_map/pallas_call | solution.py:553
  24.4 0.6 %copy.6 = f32[4,2,128]{2,1,0:T(2,128)} copy(f32[4,2,128]{2,1,0:T(2,128)S(1)} %bitcast.1) | data formatting | bytes 8192
where the time goes:
time: 25.2 us; the launch traced here: 25 us
  Pallas kernels  24.4 us (97%)
  local copies, waits for them, and re-layouts  0.6 us (2%)
    pallas_call x1, Pallas kernels, on_device(): pl.pallas_call(functools.partial(kernel, lights, views), out_shape=pltpu....  24.4 us
    unnamed x1, local copies, waits for them, and re-layouts  0.6 us

commit v1 on v0

--- a/solution.py
+++ b/solution.py
@@ -532,10 +532,431 @@
             first_on(s).wait_send()
 
 
+def column_kernel(
+    lights,
+    views,
+    halo,
+    density_hbm,
+    colour_hbm,
+    absorb_ref,
+    light_hbm,
+    out_ref,
+    dens_rows,
+    light_rows,
+    colour_rows,
+    colour_wide,
+    dens_ring,
+    light_ring,
+    dens_in,
+    light_in,
+    colour_in,
+    first_in,
+    dens_op,
+    first_op,
+    inside_ref,
+    planes,
+    lit,
+    weight,
+    chain_in,
+    chain_out,
+    load_sem,
+    dens_send,
+    dens_recv,
+    ring_send,
+    ring_recv,
+    light_send,
+    light_recv,
+    seam_send,
+    seam_recv,
+    colour_send,
+    colour_recv,
+    first_send,
+    first_recv,
+    chain_send,
+    chain_recv,
+):
+    l = lax.axis_index("light")
+    v = lax.axis_index("view")
+    slices, height, width = dens_rows.shape
+    channels = light_rows.shape[0]
+    cols = width // views
+    tall = views * height
+    wide = cols + 2 * halo
+    f32 = jnp.float32
+    has_next = l < lights - 1
+
+    barrier = pltpu.get_barrier_semaphore()
+
+    def greet(to_l, to_v):
+        pl.semaphore_signal(
+            barrier, inc=1, device_id={"light": to_l, "view": to_v}, device_id_type=MESH
+        )
+
+    for step in range(1, views):
+        greet(l, lax.rem(v + step, views))
+
+    @pl.when(l == 1)
+    def _():
+        for step in range(views):
+            greet(l - 1, lax.rem(v + step, views))
+
+    @pl.when(l > 1)
+    def _():
+        greet(l - 1, v)
+
+    loads = [
+        pltpu.make_async_copy(src, dst, load_sem.at[i])
+        for i, (src, dst) in enumerate(
+            ((density_hbm, dens_rows), (light_hbm, light_rows), (colour_hbm, colour_rows))
+        )
+    ]
+    for load in loads:
+        load.start()
+
+    def block(b):
+        return slice(b * cols, (b + 1) * cols)
+
+    lane = lax.broadcasted_iota(jnp.int32, (height, cols), 1)
+
+    def build_ring(ring, rows):
+        for b in range(views):
+            tile = jnp.zeros((height, cols), f32)
+            for k in range(rows.shape[0]):
+                start = 2 * halo * k
+                right = rows[k, :, block((b + 1) % views)]
+                left = rows[k, :, block((b - 1) % views)]
+                if start:
+                    right = pltpu.roll(right, start, 1)
+                    left = pltpu.roll(left, start, 1)
+                low = (start - halo) % cols
+                tile = jnp.where((lane >= start) & (lane < start + halo), right, tile)
+                tile = jnp.where((lane >= low) & (lane < low + halo), left, tile)
+            ring[b] = tile
+
+    loads[0].wait()
+    build_ring(dens_ring, dens_rows)
+    loads[1].wait()
+
+    @pl.when(l <= 1)
+    def _():
+        build_ring(light_ring, light_rows)
+
+    zero = jnp.int32(0)
+    others = jnp.where(l == 0, jnp.int32(views), jnp.where(has_next, jnp.int32(1), zero))
+    pl.semaphore_wait(barrier, views - 1 + others)
+
+    def aim(step):
+        target = lax.rem(v + step, views)
+        return target, pl.ds(pl.multiple_of(target * cols, cols), cols)
+
+    here = pl.ds(pl.multiple_of(v * height, height), height)
+
+    def copy(src, dst, send, recv, to_l, to_v):
+        return pltpu.make_async_remote_copy(
+            src_ref=src,
+            dst_ref=dst,
+            send_sem=send,
+            recv_sem=recv,
+            device_id={"light": to_l, "view": to_v},
+            device_id_type=MESH,
+        )
+
+    def move(src, dst, sends, recvs, step, target):
+        if step == 0:
+            return pltpu.make_async_copy(src, dst, recvs.at[0])
+        return copy(src, dst, sends.at[step], recvs.at[step], l, target)
+
+    def dens_move(step):
+        target, there = aim(step)
+        return move(
+            density_hbm.at[:, :, there], dens_in.at[:slices, here, :], dens_send, dens_recv, step, target
+        )
+
+    def ring_move(step):
+        target, there = aim(step)
+        return move(dens_ring.at[target], dens_in.at[slices, here, :], ring_send, ring_recv, step, target)
+
+    def light_move(step):
+        target, there = aim(step)
+        return move(
+            light_hbm.at[:, :, there], light_in.at[:channels, here, :], light_send, light_recv, step, target
+        )
+
+    def seam_move(step):
+        target, there = aim(step)
+        return move(light_ring.at[target], light_in.at[channels, here, :], seam_send, seam_recv, step, target)
+
+    def colour_move(step):
+        target, there = aim(step)
+        return move(colour_wide.at[:, :, there], colour_in.at[:, here, :], colour_send, colour_recv, step, target)
+
+    def first_move(s, step):
+        target, there = aim(step)
+        src = dens_ring.at[target] if s == slices else density_hbm.at[s, :, there]
+        return copy(
+            src, first_in.at[s, here, :], first_send.at[s, step], first_recv.at[s, step], l + 1, target
+        )
+
+    def chain_move(c):
+        return copy(chain_out.at[c], chain_in.at[c], chain_send.at[c], chain_recv.at[c], l + 1, v)
+
+    @pl.when(l == 0)
+    def _():
+        for s in (slices, *range(slices)):
+            for step in range(views):
+                first_move(s, step).start()
+
+    @pl.when(l <= 1)
+    def _():
+        for step in range(views):
+            seam_move(step).start()
+            light_move(step).start()
+
+    for step in range(views):
+        ring_move(step).start()
+        dens_move(step).start()
+
+    loads[2].wait()
+    for c in range(channels):
+        for s in range(slices):
+            colour_wide[c * slices + s] = colour_rows[c, s].astype(f32)
+    for step in range(views):
+        colour_move(step).start()
+
+    def wait_all(move_of):
+        for step in range(views):
+            if step == 0:
+                move_of(step).wait()
+            else:
+                move_of(step).wait_recv()
+
+    def place(dst, plane, ring, k):
+        start = 2 * halo * k
+        low = (start - halo) % cols
+        dst[:halo, :] = ring[low : low + halo]
+        dst[halo : halo + cols, :] = plane
+        dst[halo + cols :, :] = ring[start : start + halo]
+
+    ring_row = lax.broadcasted_iota(jnp.int32, (wide, tall), 0)
+    low = jnp.where(v > 0, 0, halo)
+    high = jnp.where(v < views - 1, wide, wide - halo)
+    inside_ref[...] = jnp.where((ring_row >= low) & (ring_row < high), 1.0, 0.0)
+
+    ring_lane = lax.broadcasted_iota(jnp.int32, (wide, tall), 1)
+    not_first = ring_lane > 0
+    not_last = ring_lane < tall - 1
+
+    def blur(p):
+        across = jnp.where(not_first, pltpu.roll(p, 1, 1), 0.0) + jnp.where(
+            not_last, pltpu.roll(p, tall - 1, 1), 0.0
+        )
+        middle = blur_center * p + blur_edge * across
+        side = blur_edge * p + blur_corner * across
+        return middle + (pltpu.roll(side, 1, 0) + pltpu.roll(side, wide - 1, 0))
+
+    def opacities(dst, src, ring, s):
+        place(dst.at[s], src[s].T, ring, s)
+        dst[s] = inside_ref[...] * opacity_of(dst[s])
+
+    def pass_slice(plane, opacity, decay):
+        return blur(plane * (inside_ref[...] - decay * opacity))
+
+    row8 = lax.broadcasted_iota(jnp.int32, (out_ref.shape[0], tall), 0)
+    lane8 = lax.broadcasted_iota(jnp.int32, (out_ref.shape[0], tall), 1)
+
+    def gather(items):
+        picks = []
+        parts = []
+        for value, pick in items:
+            large = value.astype(jnp.bfloat16)
+            small = (value - large.astype(f32)).astype(jnp.bfloat16)
+            pick = jnp.where(pick, 1.0, 0.0).astype(jnp.bfloat16)
+            picks += [pick, pick]
+            parts += [large, small]
+        return lax.dot_general(
+            jnp.concatenate(picks, axis=1),
+            jnp.concatenate(parts, axis=1),
+            (((1,), (1,)), ((), ())),
+            preferred_element_type=f32,
+        )
+
+    def own_opacity():
+        wait_all(ring_move)
+        wait_all(dens_move)
+        ring = dens_in[slices].T
+        for s in range(slices):
+            opacities(dens_op, dens_in, ring, s)
+
+    def weights():
+        y = lax.broadcasted_iota(jnp.int32, (cols, tall), 1)
+        shade = []
+        bases = []
+        for s in range(slices):
+            alpha = view_scale * dens_op[s, halo : halo + cols, :]
+            run = 1.0 - alpha
+            reach = 1
+            while reach < tall:
+                run = run * jnp.where(y >= reach, pltpu.roll(run, reach, 1), 1.0)
+                reach *= 2
+            before = jnp.where(y >= 1, pltpu.roll(run, 1, 1), 1.0)
+            bases.append(before * alpha)
+            shade.append((1.0 - run, (row8 == channels * slices + s) & (lane8 == tall - 1)))
+        out_ref[...] = gather(shade)
+        wait_all(colour_move)
+        for s in range(slices):
+            for c in range(channels):
+                weight[c, s] = bases[s] * colour_in[c * slices + s].T
+
+    def composite(c):
+        out_ref[...] += gather(
+            [(weight[c, s] * lit[c, s], row8 == c * slices + s) for s in range(slices)]
+        )
+
+    @pl.when(l <= 1)
+    def _():
+        wait_all(seam_move)
+        wait_all(light_move)
+        ring = light_in[channels].T
+        for c in range(channels):
+            place(planes.at[c], light_in[c].T, ring, c)
+
+    @pl.when(l == 1)
+    def _():
+        for s in (slices, 0):
+            for step in range(views):
+                first_move(s, step).wait_recv()
+        ring = first_in[slices].T
+        for s in range(slices):
+            if s > 0:
+                for step in range(views):
+                    first_move(s, step).wait_recv()
+            opacities(first_op, first_in, ring, s)
+            if s < slices - 1:
+                for c in range(channels):
+                    planes[c] = pass_slice(planes[c], first_op[s], absorb_ref[c])
+        own_opacity()
+
+    @pl.when(l != 1)
+    def _():
+        own_opacity()
+        weights()
+
+    for c in range(channels):
+        decay = absorb_ref[c]
+
+        @pl.when(l == 1)
+        def _():
+            planes[c] = pass_slice(planes[c], first_op[slices - 1], decay)
+
+        @pl.when(l > 1)
+        def _():
+            chain_move(c).wait_recv()
+            planes[c] = chain_in[c]
+
+        plane = planes[c]
+        for s in range(slices):
+            lit[c, s] = plane[halo : halo + cols, :]
+            if s < slices - 1:
+                plane = pass_slice(plane, dens_op[s], decay)
+
+        @pl.when((l >= 1) & has_next)
+        def _():
+            chain_out[c] = pass_slice(plane, dens_op[slices - 1], decay)
+            chain_move(c).start()
+
+        @pl.when(l != 1)
+        def _():
+            composite(c)
+
+    @pl.when(l == 1)
+    def _():
+        weights()
+        for c in range(channels):
+            composite(c)
+
+    for step in range(1, views):
+        dens_move(step).wait_send()
+        ring_move(step).wait_send()
+        colour_move(step).wait_send()
+
+    @pl.when(l <= 1)
+    def _():
+        for step in range(1, views):
+            light_move(step).wait_send()
+            seam_move(step).wait_send()
+
+    @pl.when(l == 0)
+    def _():
+        for s in range(slices + 1):
+            for step in range(views):
+                first_move(s, step).wait_send()
+
+    @pl.when((l >= 1) & has_next)
+    def _():
+        for c in range(channels):
+            chain_move(c).wait_send()
+
+
+def by_columns(lights, views, halo, density, colour, absorb, light_in):
+    slices, height, width = density.shape
+    channels = light_in.shape[0]
+    cols = width // views
+    tall = views * height
+    wide = cols + 2 * halo
+    rows = (channels + 1) * slices
+    f32 = jnp.float32
+    dma = pltpu.SemaphoreType.DMA
+    hbm = pl.BlockSpec(memory_space=pl.ANY)
+    ring = pltpu.VMEM((views, height, cols), f32)
+    spread = pltpu.VMEM((slices + 1, tall, cols), f32)
+    opacity = pltpu.VMEM((slices, wide, tall), f32)
+    lights3 = pltpu.VMEM((channels, wide, tall), f32)
+    voxels = pltpu.VMEM((channels, slices, cols, tall), f32)
+    image = pl.pallas_call(
+        functools.partial(column_kernel, lights, views, halo),
+        out_shape=pltpu.VMEM((rows, cols), f32),
+        in_specs=[hbm, hbm, pl.BlockSpec(memory_space=pltpu.SMEM), hbm],
+        out_specs=pl.BlockSpec(memory_space=pltpu.VMEM),
+        scratch_shapes=[
+            pltpu.VMEM(density.shape, density.dtype),
+            pltpu.VMEM(light_in.shape, light_in.dtype),
+            pltpu.VMEM(colour.shape, colour.dtype),
+            pltpu.VMEM((channels * slices, height, width), f32),
+            ring,
+            ring,
+            spread,
+            pltpu.VMEM((channels + 1, tall, cols), f32),
+            pltpu.VMEM((channels * slices, tall, cols), f32),
+            spread,
+            opacity,
+            opacity,
+            pltpu.VMEM((wide, tall), f32),
+            lights3,
+            voxels,
+            voxels,
+            lights3,
+            lights3,
+            dma((3,)),
+            *[dma((views,))] * 10,
+            dma((slices + 1, views)),
+            dma((slices + 1, views)),
+            dma((channels,)),
+            dma((channels,)),
+        ],
+        compiler_params=pltpu.CompilerParams(collective_id=0, has_side_effects=True),
+    )(density, colour, absorb, light_in)
+    return image.reshape(channels + 1, slices, cols)
+
+
 def on_device(lights, views, density, colour, absorb, light_in):
     slices, height, width = density.shape
     channels = light_in.shape[0]
     cols = width // views
+    halo = -(-(lights * slices - 1) // 8) * 8
+    whole_tiles = cols % 128 == 0 and views * height == 128 and height % 8 == 0
+    packs = 2 * halo * max(channels, slices) <= cols
+    if lights > 1 and whole_tiles and packs:
+        return by_columns(lights, views, halo, density, colour, absorb, light_in)
     rows = (channels + 1) * slices
     spare = -(-4 * slices // 8) * 8
     reach2 = 2 * slices

time: 25.2 us -> 25 us (level)
  no operation moved by 1% of the time
where the time goes in v1:
time: 25 us; the launch traced here: 24.8 us
  Pallas kernels  24.2 us (97%)
  local copies, waits for them, and re-layouts  0.6 us (2%)
    pallas_call x1, Pallas kernels, by_columns(): pl.pallas_call(functools.partial(column_kernel, lights, views, halo), out...  24.2 us
    unnamed x1, local copies, waits for them, and re-layouts  0.6 us

profile of v1, /device:TPU:25, one launch (start us, length us, event | category | flops | bytes accessed | tf_op | source)
XLA Modules:
  0.0 24.8 jit_solution(8881936558933392207)
XLA Ops:
  0.0 24.2 %shard_map.46 = f32[8,128]{1,0:T(8,128)S(1)} custom-call(f32[2,16,1024]{2,1,0:T(8,128)} %density_hbm.1, bf16[3,2,16,1024]{3,2,1,0:T(8,128)(2,1)} %colour_hbm.1, f32[3]{0:T(128)} %absorb_ref.1, f32[3,16,1024]{2,1,0:T(8,128)} %light_hbm.1), custom_call_target="tpu_custom_call" | custom-call | tf_op jit(solution)/shard_map/pallas_call | solution.py:915
  24.2 0.6 %copy.6 = f32[4,2,128]{2,1,0:T(2,128)} copy(f32[4,2,128]{2,1,0:T(2,128)S(1)} %bitcast.1) | data formatting | bytes 8192

commit v2 on v1

--- a/solution.py
+++ b/solution.py
@@ -550,7 +550,6 @@
     dens_in,
     light_in,
     colour_in,
-    first_in,
     dens_op,
     first_op,
     inside_ref,
@@ -595,12 +594,7 @@
     for step in range(1, views):
         greet(l, lax.rem(v + step, views))
 
-    @pl.when(l == 1)
-    def _():
-        for step in range(views):
-            greet(l - 1, lax.rem(v + step, views))
-
-    @pl.when(l > 1)
+    @pl.when(l > 0)
     def _():
         greet(l - 1, v)
 
@@ -633,17 +627,7 @@
                 tile = jnp.where((lane >= low) & (lane < low + halo), left, tile)
             ring[b] = tile
 
-    loads[0].wait()
-    build_ring(dens_ring, dens_rows)
-    loads[1].wait()
-
-    @pl.when(l <= 1)
-    def _():
-        build_ring(light_ring, light_rows)
-
-    zero = jnp.int32(0)
-    others = jnp.where(l == 0, jnp.int32(views), jnp.where(has_next, jnp.int32(1), zero))
-    pl.semaphore_wait(barrier, views - 1 + others)
+    pl.semaphore_wait(barrier, views - 1 + jnp.where(has_next, jnp.int32(1), jnp.int32(0)))
 
     def aim(step):
         target = lax.rem(v + step, views)
@@ -666,10 +650,10 @@
             return pltpu.make_async_copy(src, dst, recvs.at[0])
         return copy(src, dst, sends.at[step], recvs.at[step], l, target)
 
-    def dens_move(step):
+    def dens_move(s, step):
         target, there = aim(step)
         return move(
-            density_hbm.at[:, :, there], dens_in.at[:slices, here, :], dens_send, dens_recv, step, target
+            density_hbm.at[s, :, there], dens_in.at[s, here, :], dens_send.at[s], dens_recv.at[s], step, target
         )
 
     def ring_move(step):
@@ -690,31 +674,43 @@
         target, there = aim(step)
         return move(colour_wide.at[:, :, there], colour_in.at[:, here, :], colour_send, colour_recv, step, target)
 
-    def first_move(s, step):
-        target, there = aim(step)
-        src = dens_ring.at[target] if s == slices else density_hbm.at[s, :, there]
-        return copy(
-            src, first_in.at[s, here, :], first_send.at[s, step], first_recv.at[s, step], l + 1, target
-        )
+    def first_move(s):
+        return copy(dens_op.at[s], first_op.at[s], first_send.at[s], first_recv.at[s], l + 1, v)
 
     def chain_move(c):
         return copy(chain_out.at[c], chain_in.at[c], chain_send.at[c], chain_recv.at[c], l + 1, v)
 
-    @pl.when(l == 0)
-    def _():
-        for s in (slices, *range(slices)):
-            for step in range(views):
-                first_move(s, step).start()
-
-    @pl.when(l <= 1)
-    def _():
+    @pl.when(l == 1)
+    def _():
+        for step in range(views):
+            light_move(step).start()
+
+    for step in range(views):
+        dens_move(0, step).start()
+
+    loads[1].wait()
+
+    @pl.when(l == 1)
+    def _():
+        build_ring(light_ring, light_rows)
         for step in range(views):
             seam_move(step).start()
-            light_move(step).start()
-
+
+    loads[0].wait()
+    build_ring(dens_ring, dens_rows)
     for step in range(views):
         ring_move(step).start()
-        dens_move(step).start()
+    for s in range(1, slices):
+        for step in range(views):
+            dens_move(s, step).start()
+
+    @pl.when(l == 0)
+    def _():
+        for step in range(views):
+            light_move(step).start()
+        build_ring(light_ring, light_rows)
+        for step in range(views):
+            seam_move(step).start()
 
     loads[2].wait()
     for c in range(channels):
@@ -782,10 +778,14 @@
 
     def own_opacity():
         wait_all(ring_move)
-        wait_all(dens_move)
         ring = dens_in[slices].T
         for s in range(slices):
+            wait_all(functools.partial(dens_move, s))
             opacities(dens_op, dens_in, ring, s)
+
+            @pl.when(l == 0)
+            def _():
+                first_move(s).start()
 
     def weights():
         y = lax.broadcasted_iota(jnp.int32, (cols, tall), 1)
@@ -812,8 +812,7 @@
             [(weight[c, s] * lit[c, s], row8 == c * slices + s) for s in range(slices)]
         )
 
-    @pl.when(l <= 1)
-    def _():
+    def gather_light():
         wait_all(seam_move)
         wait_all(light_move)
         ring = light_in[channels].T
@@ -822,24 +821,25 @@
 
     @pl.when(l == 1)
     def _():
-        for s in (slices, 0):
-            for step in range(views):
-                first_move(s, step).wait_recv()
-        ring = first_in[slices].T
-        for s in range(slices):
-            if s > 0:
-                for step in range(views):
-                    first_move(s, step).wait_recv()
-            opacities(first_op, first_in, ring, s)
-            if s < slices - 1:
-                for c in range(channels):
-                    planes[c] = pass_slice(planes[c], first_op[s], absorb_ref[c])
-        own_opacity()
+        gather_light()
+        for s in range(slices - 1):
+            first_move(s).wait_recv()
+            for c in range(channels):
+                planes[c] = pass_slice(planes[c], first_op[s], absorb_ref[c])
+
+    own_opacity()
+
+    @pl.when(l == 1)
+    def _():
+        first_move(slices - 1).wait_recv()
 
     @pl.when(l != 1)
     def _():
-        own_opacity()
         weights()
+
+    @pl.when(l == 0)
+    def _():
+        gather_light()
 
     for c in range(channels):
         decay = absorb_ref[c]
@@ -875,7 +875,8 @@
             composite(c)
 
     for step in range(1, views):
-        dens_move(step).wait_send()
+        for s in range(slices):
+            dens_move(s, step).wait_send()
         ring_move(step).wait_send()
         colour_move(step).wait_send()
 
@@ -887,9 +888,8 @@
 
     @pl.when(l == 0)
     def _():
-        for s in range(slices + 1):
-            for step in range(views):
-                first_move(s, step).wait_send()
+        for s in range(slices):
+            first_move(s).wait_send()
 
     @pl.when((l >= 1) & has_next)
     def _():
@@ -927,7 +927,6 @@
             spread,
             pltpu.VMEM((channels + 1, tall, cols), f32),
             pltpu.VMEM((channels * slices, tall, cols), f32),
-            spread,
             opacity,
             opacity,
             pltpu.VMEM((wide, tall), f32),
@@ -937,9 +936,11 @@
             lights3,
             lights3,
             dma((3,)),
-            *[dma((views,))] * 10,
-            dma((slices + 1, views)),
-            dma((slices + 1, views)),
+            dma((slices, views)),
+            dma((slices, views)),
+            *[dma((views,))] * 8,
+            dma((slices,)),
+            dma((slices,)),
             dma((channels,)),
             dma((channels,)),
         ],

time: 25 us -> 24 us (0.960)
  the two profiles are of different devices: /device:TPU:25 before, /device:TPU:28 now
where the time goes in v2:
time: 24 us; the launch traced here: 23.9 us
  Pallas kernels  23.3 us (97%)
  local copies, waits for them, and re-layouts  0.6 us (2%)
    pallas_call x1, Pallas kernels, by_columns(): pl.pallas_call(functools.partial(column_kernel, lights, views, halo), out...  23.3 us
    unnamed x1, local copies, waits for them, and re-layouts  0.6 us

profile of v2, /device:TPU:28, one launch (start us, length us, event | category | flops | bytes accessed | tf_op | source)
XLA Modules:
  0.0 23.9 jit_solution(2663810762461545584)
XLA Ops:
  0.0 23.3 %shard_map.46 = f32[8,128]{1,0:T(8,128)S(1)} custom-call(f32[2,16,1024]{2,1,0:T(8,128)} %density_hbm.1, bf16[3,2,16,1024]{3,2,1,0:T(8,128)(2,1)} %colour_hbm.1, f32[3]{0:T(128)} %absorb_ref.1, f32[3,16,1024]{2,1,0:T(8,128)} %light_hbm.1), custom_call_target="tpu_custom_call" | custom-call | tf_op jit(solution)/shard_map/pallas_call | solution.py:915
  23.3 0.6 %copy.6 = f32[4,2,128]{2,1,0:T(2,128)} copy(f32[4,2,128]{2,1,0:T(2,128)S(1)} %bitcast.1) | data formatting | bytes 8192
